TPU v7x, 128 devices: a whole 4x4x4 slice. The times are simulated.
128 devices in a mesh: sec: 2 (over y_lo), dp: 16 (over z, y_hi, core), tensor: 4 (over x).
Axes of the slice: x: 4, y: 4 (y_hi: 2, y_lo: 2; y = y_hi * 2 + y_lo), z: 4, core: 2. Of those that a mesh axis runs over, the one named last changes fastest.
Arguments:
- student_rows: bfloat16 [2, 8192, 5376], P('sec', 'dp'), may hold values from -24 to 24
- teacher_rows: bfloat16 [2, 8192, 5376], P('sec', 'dp'), may hold values from -6 to 6
- norm_gain: float32 [5376], replicated, may hold values from 0.5 to 1.5
- post_gain: float32 [5376], replicated, may hold values from 0.5 to 1.5
- query_weight: bfloat16 [5376, 2048], P(('sec', 'dp'), 'tensor')
- key_weight: bfloat16 [5376, 1024], P(('sec', 'dp'), 'tensor')
- value_weight: bfloat16 [5376, 1024], P(('sec', 'dp'), 'tensor'), may hold values from -0.078125 to 0.078125
- out_weight: bfloat16 [5376, 2048], P(('sec', 'dp'), 'tensor'), may hold values from -0.125 to 0.125
Outputs:
- layer_output: bfloat16 [2, 8192, 5376], P('sec', 'dp', 'tensor')
- query_grad: float32 [5376, 2048], P(('sec', 'dp'), 'tensor')
- output_grad: float32 [5376, 2048], P(('sec', 'dp'), 'tensor')
All inputs are finite; a program needn't handle non-finite values.
Results may differ from a plain program's by a relative error of at most 0.025.
The roundings to bfloat16 on the way count: a program that leaves them out, or rounds other values in their place, can miss the bound.
Values may be sent and summed in bfloat16 or wider, within the bound.
A program may use at most 128 MiB of HBM per device.

v0:
```python
import math
import jax
import jax.numpy as jnp
from jax import lax
from jax.sharding import PartitionSpec as P

HEADS = 8
KV_HEADS = 4
HD = 256
W = 1024
norm_eps = 1e-06
rope_base = 10000.0
masked_score = -1e30


def from_partner(block, axis, bit):
    count = lax.axis_size(axis)
    route = []
    for low in range(count):
        high = low | 1 << bit
        if high != low and high < count:
            route += [(low, high), (high, low)]
    return lax.ppermute(block, axis, route)


def from_behind(x, axis, by):
    count = lax.axis_size(axis)
    pairs = [(i, i + by) for i in range(count) if 0 <= i + by < count]
    return lax.ppermute(x, axis, pairs)


def rotate(values, cos_table, sin_table, sign_value):
    row_count = values.shape[0]
    half_dim = cos_table.shape[1]
    per_head = values.reshape(row_count, -1, 2 * half_dim)
    leading = per_head[:, :, :half_dim]
    trailing = per_head[:, :, half_dim:]
    cosines = cos_table[:, None, :]
    sin_scaled = sign_value * sin_table[:, None, :]
    rotated = jnp.concatenate(
        [leading * cosines - trailing * sin_scaled, trailing * cosines + leading * sin_scaled],
        axis=2,
    )
    return rotated.reshape(row_count, -1)


def shards(
    student_rows,
    teacher_rows,
    norm_gain,
    post_gain,
    query_weight,
    key_weight,
    value_weight,
    out_weight,
):
    tok_count = student_rows.shape[1]
    model_width = student_rows.shape[2]
    tensor_count = lax.axis_size("tensor")
    share_cols = model_width // tensor_count
    data_count = lax.axis_size("sec") * lax.axis_size("dp")
    blocks_back = (W + tok_count - 1) // tok_count
    key_count = (blocks_back + 1) * tok_count
    local_groups = key_weight.shape[1] // HD
    group_size = HEADS // KV_HEADS
    query_cols = query_weight.shape[1]
    score_scale = 1.0 / math.sqrt(HD)
    loss_scale = 2.0 / math.sqrt(data_count * tok_count)
    target = from_partner(teacher_rows[0], "sec", 0)
    query_full, key_full, value_full, out_full = (
        lax.all_gather(query_weight, ("sec", "dp"), axis=0, tiled=True),
        lax.all_gather(key_weight, ("sec", "dp"), axis=0, tiled=True),
        lax.all_gather(value_weight, ("sec", "dp"), axis=0, tiled=True),
        lax.all_gather(out_weight, ("sec", "dp"), axis=0, tiled=True),
    )
    student_f = student_rows[0].astype(jnp.float32)
    inverse = lax.rsqrt(jnp.mean(student_f * student_f, axis=1, keepdims=True) + norm_eps)
    normed = (student_f * inverse * norm_gain).astype(jnp.bfloat16)
    first_pos = lax.axis_index("dp") * tok_count
    half_dim = HD // 2
    inv_freq = jnp.power(
        jnp.float32(rope_base), -2.0 * jnp.arange(half_dim, dtype=jnp.float32) / HD
    )
    positions = (first_pos + jnp.arange(tok_count, dtype=jnp.int32)).astype(jnp.float32)
    angles = positions[:, None] * inv_freq[None, :]
    cos_table = jnp.cos(angles)
    sin_table = jnp.sin(angles)
    queries = rotate(
        jnp.dot(normed, query_full, preferred_element_type=jnp.float32), cos_table, sin_table, 1.0
    ).astype(jnp.bfloat16)
    key_rows = rotate(
        jnp.dot(normed, key_full, preferred_element_type=jnp.float32), cos_table, sin_table, 1.0
    ).astype(jnp.bfloat16)
    value_rows = jnp.dot(normed, value_full, preferred_element_type=jnp.float32).astype(
        jnp.bfloat16
    )
    key_parts = [key_rows]
    value_parts = [value_rows]
    for offset in range(1, blocks_back + 1):
        earlier_keys, earlier_values = from_behind((key_rows, value_rows), "dp", offset)
        key_parts = [earlier_keys] + key_parts
        value_parts = [earlier_values] + value_parts
    key_window = jnp.concatenate(key_parts, axis=0)
    value_window = jnp.concatenate(value_parts, axis=0)
    query_pos = first_pos + jnp.arange(tok_count, dtype=jnp.int32)
    key_pos = first_pos - blocks_back * tok_count + jnp.arange(key_count, dtype=jnp.int32)
    allowed = (
        (key_pos[None, :] >= 0)
        & (key_pos[None, :] <= query_pos[:, None])
        & (key_pos[None, :] > query_pos[:, None] - W)
    )
    grouped_q = queries.reshape(tok_count, local_groups, group_size, HD)
    grouped_k = key_window.reshape(key_count, local_groups, HD)
    grouped_v = value_window.reshape(key_count, local_groups, HD)
    scores = (
        jnp.einsum("tgad,kgd->gatk", grouped_q, grouped_k, preferred_element_type=jnp.float32)
        * score_scale
    )
    scores = jnp.where(allowed, scores, masked_score)
    row_peak = jnp.max(scores, axis=3, keepdims=True)
    exp_scores = jnp.exp(scores - row_peak)
    attn_probs = exp_scores / jnp.sum(exp_scores, axis=3, keepdims=True)
    probs_b = attn_probs.astype(jnp.bfloat16)
    mixed_rows = (
        jnp.einsum("gatk,kgd->tgad", probs_b, grouped_v, preferred_element_type=jnp.float32)
        .astype(jnp.bfloat16)
        .reshape(tok_count, query_cols)
    )
    partial_value = jnp.einsum(
        "te,de->td", mixed_rows, out_full, preferred_element_type=jnp.float32
    )
    summed = lax.psum(partial_value.astype(jnp.bfloat16), "tensor").astype(jnp.float32)
    post_factor = lax.rsqrt(jnp.mean(summed * summed, axis=1, keepdims=True) + norm_eps)
    layer_full = (student_f + summed * post_factor * post_gain).astype(jnp.bfloat16)
    loss_grad = loss_scale * (layer_full.astype(jnp.float32) - target.astype(jnp.float32))
    scaled = post_gain * loss_grad
    along_sum = jnp.mean(summed * scaled, axis=1, keepdims=True)
    pre_grad = (
        post_factor * scaled - summed * post_factor * post_factor * post_factor * along_sum
    ).astype(jnp.bfloat16)
    mixed_grad = jnp.dot(pre_grad, out_full, preferred_element_type=jnp.float32).astype(
        jnp.bfloat16
    )
    grouped_g = mixed_grad.reshape(tok_count, local_groups, group_size, HD)
    prob_grad = jnp.einsum(
        "tgad,kgd->gatk", grouped_g, grouped_v, preferred_element_type=jnp.float32
    )
    score_grad = (
        attn_probs * (prob_grad - jnp.sum(attn_probs * prob_grad, axis=3, keepdims=True))
    ).astype(jnp.bfloat16)
    rotated_grad = (
        jnp.einsum(
            "gatk,kgd->tgad", score_grad, grouped_k, preferred_element_type=jnp.float32
        ).reshape(tok_count, query_cols)
        * score_scale
    )
    query_pre = rotate(rotated_grad, cos_table, sin_table, -1.0).astype(jnp.bfloat16)
    query_term = jnp.einsum("td,te->de", normed, query_pre, preferred_element_type=jnp.float32)
    out_term = jnp.einsum("td,te->de", pre_grad, mixed_rows, preferred_element_type=jnp.float32)
    grad_owned = lax.psum_scatter(
        jnp.concatenate([query_term, out_term], axis=1).astype(jnp.bfloat16),
        ("sec", "dp"),
        scatter_dimension=0,
        tiled=True,
    ).astype(jnp.float32)
    layer_share = lax.dynamic_slice_in_dim(
        layer_full, lax.axis_index("tensor") * share_cols, share_cols, 1
    )
    return (layer_share[None], grad_owned[:, :query_cols], grad_owned[:, query_cols:])


def solution(mesh):
    in_specs = (
        P("sec", "dp", None),
        P("sec", "dp", None),
        P(),
        P(),
        P(("sec", "dp"), "tensor"),
        P(("sec", "dp"), "tensor"),
        P(("sec", "dp"), "tensor"),
        P(("sec", "dp"), "tensor"),
    )
    out_specs = (P("sec", "dp", "tensor"), P(("sec", "dp"), "tensor"), P(("sec", "dp"), "tensor"))
    return jax.shard_map(shards, mesh=mesh, in_specs=in_specs, out_specs=out_specs, check_vma=False)
```

profile of v0, /device:TPU:2, one launch (start us, length us, event | category | flops | bytes accessed | tf_op | source)
XLA Modules:
  0.0 628.8 jit_solution(17924069632204809534)
XLA Ops:
  10.1 3.7 fusion.9
  16.0 53.6 %all-gather.7.cloned.1.call-done = bf16[5376,256]{1,0:T(8,128)(2,1)} async-done(((bf16[168,256]{1,0:T(8,128)(2,1)}), bf16[5376,256]{1,0:T(8,128)(2,1)}) %all-gather.7.cloned.1.call-update) | async-done | bytes 2752528 | tf_op jit(solution)/shard_map/all_gather | solution.py:72
  69.6 5.4 fusion.50
  76.2 2.1 collective-permute-start.3
  78.4 4.0 collective-permute-start.2
  82.4 53.2 %all-gather.5.cloned.1.call-done = bf16[5376,256]{1,0:T(8,128)(2,1)} async-done(((bf16[168,256]{1,0:T(8,128)(2,1)}), bf16[5376,256]{1,0:T(8,128)(2,1)}) %all-gather.5.cloned.1.call-update) | async-done | bytes 2752528 | tf_op jit(solution)/shard_map/all_gather | solution.py:73
  135.6 5.0 fusion.53
  140.7 2.1 collective-permute-start.1
  142.8 4.3 collective-permute-start
  147.1 57.4 %all-gather.9.cloned.1.call-done = bf16[5376,512]{1,0:T(8,128)(2,1)} async-done(((bf16[168,512]{1,0:T(8,128)(2,1)}), bf16[5376,512]{1,0:T(8,128)(2,1)}) %all-gather.9.cloned.1.call-update) | async-done | bytes 5505040 | tf_op jit(solution)/shard_map/all_gather | solution.py:71
  204.5 8.3 %copy.30 = bf16[512,5376]{1,0:T(8,128)(2,1)} copy(bf16[512,5376]{0,1:T(8,128)(2,1)} %bitcast.134) | data formatting | bytes 11010048 | tf_op jit(solution)/shard_map/dot_general | solution.py:89
  212.8 7.0 %fusion.22 = f32[512,2,256]{0,2,1:T(8,128)S(1)} fusion(bf16[2,256,5376]{2,1,0:T(8,128)(2,1)} %bitcast.135, bf16[1,512,5376]{2,1,0:T(8,128)(2,1)} %param.8, f32[5376]{0:T(1024)S(1)} %copy-done.4, f32[512]{0:T(512)S(1)} %add_rsqrt_fusion.1), kind=kOutput, calls=%fused_computation.36 | convolution fusion | flops 2829582336 | bytes 12082176 | tf_op jit(solution)/shard_map/dot_general | solution.py:89
  221.4 1.5 fusion.21
  224.0 3.1 fusion.47
  227.1 39.8 %all-gather.11.cloned.1.call-done = bf16[5376,512]{1,0:T(8,128)(2,1)} async-done(((bf16[168,512]{1,0:T(8,128)(2,1)}), bf16[5376,512]{1,0:T(8,128)(2,1)}) %all-gather.11.cloned.1.call-update) | async-done | bytes 5505040 | tf_op jit(solution)/shard_map/all_gather | solution.py:74
  266.9 8.3 %convolution_convert_fusion.2 = bf16[512,5376]{1,0:T(8,128)(2,1)} fusion(bf16[512,512]{0,1:T(8,128)(2,1)} %bitcast.139, bf16[5376,512]{1,0:T(8,128)(2,1)} %all-gather.11.cloned.1.call-done), kind=kOutput, calls=%fused_computation.26 | convolution fusion | flops 2821324800 | bytes 11534336 | tf_op jit(solution)/shard_map/te,de->td/dot_general | solution.py:129
  275.3 1.6 collective-permute-start.4
  276.8 110.7 %all-reduce.2.cloned.1.call-done = bf16[512,5376]{1,0:T(8,128)(2,1)} async-done(((bf16[512,5376]{1,0:T(8,128)(2,1)}), bf16[512,5376]{1,0:T(8,128)(2,1)}) %all-reduce.2.cloned.1.call-update) | async-done | bytes 5505040 | tf_op jit(solution)/shard_map/psum | solution.py:132
  387.5 3.9 fusion.15
  391.4 5.3 collective-permute-done.4
  396.7 7.1 %fusion.16 = (f32[512]{0:T(512)S(1)}, bf16[512,5376]{1,0:T(8,128)(2,1)S(1)}) fusion(bf16[512,5376]{1,0:T(8,128)(2,1)S(1)} %copy-done, bf16[512,5376]{1,0:T(8,128)(2,1)} %collective-permute-done.4, f32[5376]{0:T(1024)S(1)} %broadcast_multiply_fusion.1, f32[5376]{0:T(1024)S(1)} %copy-done.3, f32[512]{0:T(512)S(1)} %add_rsqrt_fusion, bf16[1,512,5376]{2,1,0:T(8,128)(2,1)} %param.8), kind=kLoop, calls=%fused_computation.21 | loop fusion | flops 33029632 | bytes 22067200 | tf_op jit(solution)/shard_map/reduce_sum | solution.py:137
  403.8 8.0 %fusion.8 = bf16[512,5376]{1,0:T(8,128)(2,1)S(1)} fusion(bf16[512,5376]{1,0:T(8,128)(2,1)S(1)} %copy-done, bf16[512,5376]{1,0:T(8,128)(2,1)} %collective-permute-done.4, bf16[512,5376]{1,0:T(8,128)(2,1)S(1)} %get-tuple-element.13, f32[512]{0:T(512)S(1)} %broadcast_multiply_fusion.2, f32[5376]{0:T(1024)S(1)} %broadcast_multiply_fusion.1, f32[512]{0:T(512)S(1)} %add_rsqrt_fusion), kind=kLoop, calls=%fused_computation.13 | loop fusion | flops 33030144 | bytes 22045696 | tf_op jit(solution)/shard_map/convert_element_type | solution.py:140
  411.8 3.2 convolution_convert_fusion
  415.1 5.8 convolution_convert_fusion.3
  420.9 2.3 fusion.17
  423.2 2.7 fusion.44
  426.2 3.6 convolution_convert_fusion.1
  429.9 5.1 pad_maximum_fusion
  435.0 14.7 %copy.48 = bf16[5376,1024]{1,0:T(8,128)(2,1)} copy(bf16[5376,1024]{0,1:T(8,128)(2,1)} %pad_maximum_fusion) | data formatting | bytes 22020096
  449.7 2.3 constant_dynamic-slice_fusion
  452.0 1.5 copy.35
  453.5 165.0 %reduce-scatter.4.cloned.1.call-done = bf16[168,1024]{1,0:T(8,128)(2,1)} async-done(((bf16[5376,1024]{1,0:T(8,128)(2,1)}), bf16[168,1024]{1,0:T(8,128)(2,1)}) %reduce-scatter.4.cloned.1.call-update) | async-done | bytes 344080
  (59 shorter events, 12.4 us)
Async XLA Ops:
  7.2 62.5 %copy-start.4 = (f32[5376]{0:T(1024)S(1)}, f32[5376]{0:T(1024)}, u32[]{:S(2)}) copy-start(f32[5376]{0:T(1024)} %param.10) | copy-start | bytes 64516
  7.2 62.5 %all-gather.7.cloned.1.call-start = ((), (), s32[]{:S(2)}) async-start(), calls=%async_computation.2 | async-start | bytes 2838528 | tf_op jit(solution)/shard_map/all_gather | solution.py:72
  7.9 127.7 %all-gather.5.cloned.1.call-start = ((), (), s32[]{:S(2)}) async-start(), calls=%async_computation.1 | async-start | bytes 2838528 | tf_op jit(solution)/shard_map/all_gather | solution.py:73
  8.7 195.8 %all-gather.9.cloned.1.call-start = ((), (), s32[]{:S(2)}) async-start(), calls=%async_computation.3 | async-start | bytes 5677056 | tf_op jit(solution)/shard_map/all_gather | solution.py:71
  9.4 257.5 %all-gather.11.cloned.1.call-start = ((), (), s32[]{:S(2)}) async-start(), calls=%async_computation.4 | async-start | bytes 5677056 | tf_op jit(solution)/shard_map/all_gather | solution.py:74
  10.0 377.5 %all-reduce.2.cloned.1.call-start = ((), (), s32[]{:S(2)}) async-start(), calls=%async_computation.5 | async-start | bytes 11010048 | tf_op jit(solution)/shard_map/psum | solution.py:132
  76.2 143.7 %collective-permute-start.3 = (bf16[512,256]{0,1:T(8,128)(2,1)S(1)}, bf16[512,256]{0,1:T(8,128)(2,1)S(1)}, u32[]{:S(2)}, u32[]{:S(2)}) collective-permute-start(bf16[512,256]{0,1:T(8,128)(2,1)S(1)} %maximum_bitcast_fusion.6), channel_id=1, source_target_pairs={{0,4},{4,8},{8,12},{12,16},{16,20},{20,24},{24,28},{28,32},{32,36}... | collective-permute-start | bytes 786440 | tf_op jit(solution)/shard_map/ppermute | solution.py:29
  78.4 141.6 %collective-permute-start.2 = (bf16[512,256]{0,1:T(8,128)(2,1)S(1)}, bf16[512,256]{0,1:T(8,128)(2,1)S(1)}, u32[]{:S(2)}, u32[]{:S(2)}) collective-permute-start(bf16[512,256]{0,1:T(8,128)(2,1)S(1)} %maximum_bitcast_fusion.6), channel_id=1, source_target_pairs={{0,8},{4,12},{8,16},{12,20},{16,24},{20,28},{24,32},{28,36},{32,40... | collective-permute-start | bytes 786440 | tf_op jit(solution)/shard_map/ppermute | solution.py:29
  140.7 82.2 %collective-permute-start.1 = (bf16[512,256]{1,0:T(8,128)(2,1)S(1)}, bf16[512,256]{1,0:T(8,128)(2,1)S(1)}, u32[]{:S(2)}, u32[]{:S(2)}) collective-permute-start(bf16[512,256]{1,0:T(8,128)(2,1)S(1)} %fusion.53), channel_id=1, source_target_pairs={{0,4},{4,8},{8,12},{12,16},{16,20},{20,24},{24,28},{28,32},{32,36}... | collective-permute-start | bytes 786440 | tf_op jit(solution)/shard_map/ppermute | solution.py:29
  142.8 80.1 %collective-permute-start = (bf16[512,256]{1,0:T(8,128)(2,1)S(1)}, bf16[512,256]{1,0:T(8,128)(2,1)S(1)}, u32[]{:S(2)}, u32[]{:S(2)}) collective-permute-start(bf16[512,256]{1,0:T(8,128)(2,1)S(1)} %fusion.53), channel_id=1, source_target_pairs={{0,8},{4,12},{8,16},{12,20},{16,24},{20,28},{24,32},{28,36},{32,40... | collective-permute-start | bytes 786440 | tf_op jit(solution)/shard_map/ppermute | solution.py:29
  221.4 2.7 copy-start.2
  266.9 9.9 %copy-start.3 = (f32[5376]{0:T(1024)S(1)}, f32[5376]{0:T(1024)}, u32[]{:S(2)}) copy-start(f32[5376]{0:T(1024)} %param.11) | copy-start | bytes 64516
  275.2 343.2 %reduce-scatter.4.cloned.1.call-start = ((), (), s32[]{:S(2)}) async-start(), calls=%async_computation.6 | async-start | bytes 11354112
  275.3 121.4 %collective-permute-start.4 = (bf16[512,5376]{1,0:T(8,128)(2,1)}, bf16[512,5376]{1,0:T(8,128)(2,1)}, u32[]{:S(2)}, u32[]{:S(2)}) collective-permute-start(bf16[512,5376]{1,0:T(8,128)(2,1)} %bitcast.138), channel_id=1, source_target_pairs={{0,64},{64,0},{1,65},{65,1},{2,66},{66,2},{3,67},{67,3},{4,68},{68... | collective-permute-start | bytes 16515080 | tf_op jit(solution)/shard_map/ppermute | solution.py:23
  387.5 9.2 %copy-start = (bf16[512,5376]{1,0:T(8,128)(2,1)S(1)}, bf16[512,5376]{1,0:T(8,128)(2,1)}, u32[]{:S(2)}) copy-start(bf16[512,5376]{1,0:T(8,128)(2,1)} %all-reduce.2.cloned.1.call-done) | copy-start | bytes 16515076
  403.8 8.0 %copy-start.1 = (bf16[512,5376]{1,0:T(8,128)(2,1)}, bf16[512,5376]{1,0:T(8,128)(2,1)S(1)}, u32[]{:S(2)}) copy-start(bf16[512,5376]{1,0:T(8,128)(2,1)S(1)} %get-tuple-element.13) | copy-start | bytes 16515076
  403.8 8.0 %copy-start.5 = (bf16[256,2,512]{2,0,1:T(8,128)(2,1)S(1)}, bf16[256,2,512]{2,0,1:T(8,128)(2,1)}, u32[]{:S(2)}) copy-start(bf16[256,2,512]{2,0,1:T(8,128)(2,1)} %fusion.47) | copy-start | bytes 1572868
  411.8 9.0 %slice-start.2 = ((s8[6291456]{0:T(1024)(128)(4,1)}), s8[4194304]{0:T(1024)(128)(4,1)S(1)}, s32[]{:S(2)}) async-start(s8[6291456]{0:T(1024)(128)(4,1)} %bitcast.132), calls=%async_computation.9 | async-start | bytes 8388608
  415.1 5.8 slice-start.3
  420.9 5.4 slice-start
  423.2 3.0 slice-start.1
Sparse Core Ops, SparseCore 0:
  9.7 59.8 all-gather.6
  71.3 64.2 all-gather.4
  137.3 67.1 all-gather.8
  206.1 60.8 all-gather.10
  275.3 112.1 all-reduce.1
  449.8 168.6 reduce-scatter.3
where the time goes:
time: 635 us; the launch traced here: 629 us
  waiting for transfers between devices  488 us (77%)
  matrix products  47.8 us (8%)
  other arithmetic  33.1 us (5%)
  local copies, waits for them, and re-layouts  31 us (5%)
  between operations  14.9 us (2%)
  starting transfers between devices  14.3 us (2%)
    unnamed x7, waiting for transfers between devices  168 us
    psum x1, waiting for transfers between devices, shards(): lax.psum(partial_value.astype(jnp.bfloat16), 'tensor').astype(jnp.float32)  111 us
    all_gather x1, waiting for transfers between devices, shards(): lax.all_gather(query_weight, ('sec', 'dp'), axis=0, tiled=True)  57.4 us
    all_gather x1, waiting for transfers between devices, shards(): lax.all_gather(key_weight, ('sec', 'dp'), axis=0, tiled=True)  53.6 us
    all_gather x1, waiting for transfers between devices, shards(): lax.all_gather(value_weight, ('sec', 'dp'), axis=0, tiled=True)  53.2 us
    all_gather x1, waiting for transfers between devices, shards(): lax.all_gather(out_weight, ('sec', 'dp'), axis=0, tiled=True)  39.8 us
    unnamed x24, local copies, waits for them, and re-layouts  18.9 us
  transfers between devices with their start and end apart: 11, of which 7 were waited for; matrix products, arithmetic and copies ran while one was open for 7% of the time, Pallas kernels for 0%

commit v1 on v0

--- a/solution.py
+++ b/solution.py
@@ -69,7 +69,12 @@
     target = from_partner(teacher_rows[0], "sec", 0)
     query_full, key_full, value_full, out_full = (
         lax.all_gather(query_weight, ("sec", "dp"), axis=0, tiled=True),
-        lax.all_gather(key_weight, ("sec", "dp"), axis=0, tiled=True),
+        jnp.concatenate(
+            lax.all_to_all(
+                jnp.stack(lax.psum(1, ("sec", "dp")) * [key_weight], axis=0), ("sec", "dp"), 0, 0
+            ),
+            0,
+        ),
         lax.all_gather(value_weight, ("sec", "dp"), axis=0, tiled=True),
         lax.all_gather(out_weight, ("sec", "dp"), axis=0, tiled=True),
     )

time: 635 us -> 590 us (0.929)
  waiting for transfers between devices: 488 us -> 439 us
  starting transfers between devices: 14.3 us -> 22.2 us
    all_gather x1 -> x0, waiting for transfers between devices: 53.6 us -> none  [shards(): lax.all_gather(key_weight, ('sec', 'dp'), axis=0, tiled=True)]
    all_to_all x0 -> x1, waiting for transfers between devices: none -> 31.8 us  [shards(): lax.all_to_all(jnp.stack(lax.psum(1, ('sec', 'dp')) * [key_weight], axis=...]
    all_gather x1, waiting for transfers between devices: 53.2 us -> 26.3 us  [shards(): lax.all_gather(value_weight, ('sec', 'dp'), axis=0, tiled=True)]
    all_to_all x0 -> x1, starting transfers between devices: none -> 8.33 us  [shards(): lax.all_to_all(jnp.stack(lax.psum(1, ('sec', 'dp')) * [key_weight], axis=...]
    unnamed x7 -> x6, waiting for transfers between devices: 168 us -> 167 us
    unnamed x24 -> x28, local copies, waits for them, and re-layouts: 18.9 us -> 18.9 us
  transfers between devices with their start and end apart: 11 -> 11, of which waited for: 7 -> 7; matrix products, arithmetic and copies ran while one was open for 7% -> 8% of each run, Pallas kernels for 0% -> 0%
where the time goes in v1:
time: 590 us; the launch traced here: 589 us
  waiting for transfers between devices  439 us (74%)
  matrix products  45.6 us (8%)
  other arithmetic  33.9 us (6%)
  local copies, waits for them, and re-layouts  33.7 us (6%)
  starting transfers between devices  22.2 us (4%)
  between operations  14.2 us (2%)
    unnamed x6, waiting for transfers between devices  167 us
    psum x1, waiting for transfers between devices, shards(): lax.psum(partial_value.astype(jnp.bfloat16), 'tensor').astype(jnp.float32)  111 us
    all_gather x1, waiting for transfers between devices, shards(): lax.all_gather(query_weight, ('sec', 'dp'), axis=0, tiled=True)  56.7 us
    all_gather x1, waiting for transfers between devices, shards(): lax.all_gather(out_weight, ('sec', 'dp'), axis=0, tiled=True)  41.6 us
    all_to_all x1, waiting for transfers between devices, shards(): lax.all_to_all(jnp.stack(lax.psum(1, ('sec', 'dp')) * [key_weight], axis=...  31.8 us
    all_gather x1, waiting for transfers between devices, shards(): lax.all_gather(value_weight, ('sec', 'dp'), axis=0, tiled=True)  26.3 us
    unnamed x28, local copies, waits for them, and re-layouts  18.9 us
    ppermute x4, starting transfers between devices, from_behind(): return lax.ppermute(x, axis, pairs)  12.2 us
  transfers between devices with their start and end apart: 11, of which 7 were waited for; matrix products, arithmetic and copies ran while one was open for 8% of the time, Pallas kernels for 0%

profile of v1, /device:TPU:2, one launch (start us, length us, event | category | flops | bytes accessed | tf_op | source)
XLA Modules:
  0.0 588.5 jit_solution(10052636917179736601)
XLA Ops:
  9.4 2.6 stack.2
  12.0 8.3 %all-to-all-start = ((bf16[32,168,256]{2,1,0:T(8,128)(2,1)}), bf16[32,168,256]{2,1,0:T(8,128)(2,1)S(1)}, u32[]{:S(2)}, u32[]{:S(2)}) async-start(bf16[32,168,256]{2,1,0:T(8,128)(2,1)} %stack.2), calls=%async_computation | async-start | bytes 5505024 | tf_op jit(solution)/shard_map/all_to_all | solution.py:73
  20.4 3.8 fusion.9
  24.2 1.8 broadcast_multiply_fusion
  27.2 31.8 %all-to-all-done = bf16[32,168,256]{2,1,0:T(8,128)(2,1)S(1)} async-done(((bf16[32,168,256]{2,1,0:T(8,128)(2,1)}), bf16[32,168,256]{2,1,0:T(8,128)(2,1)S(1)}, u32[]{:S(2)}, u32[]{:S(2)}) %all-to-all-start) | async-done | bytes 2752544 | tf_op jit(solution)/shard_map/all_to_all | solution.py:73
  59.0 4.6 fusion.50
  66.1 4.7 collective-permute-start.2
  70.8 26.3 %all-gather.4.cloned.1.call-done = bf16[5376,256]{1,0:T(8,128)(2,1)} async-done(((bf16[168,256]{1,0:T(8,128)(2,1)}), bf16[5376,256]{1,0:T(8,128)(2,1)}) %all-gather.4.cloned.1.call-update) | async-done | bytes 2752528 | tf_op jit(solution)/shard_map/all_gather | solution.py:78
  97.1 5.1 fusion.53
  102.2 2.1 collective-permute-start.1
  104.3 4.0 collective-permute-start
  108.4 56.7 %all-gather.6.cloned.1.call-done = bf16[5376,512]{1,0:T(8,128)(2,1)} async-done(((bf16[168,512]{1,0:T(8,128)(2,1)}), bf16[5376,512]{1,0:T(8,128)(2,1)}) %all-gather.6.cloned.1.call-update) | async-done | bytes 5505040 | tf_op jit(solution)/shard_map/all_gather | solution.py:71
  165.1 8.4 %copy.30 = bf16[512,5376]{1,0:T(8,128)(2,1)} copy(bf16[512,5376]{0,1:T(8,128)(2,1)} %bitcast.136) | data formatting | bytes 11010048 | tf_op jit(solution)/shard_map/dot_general | solution.py:94
  173.5 7.0 %fusion.24 = f32[512,2,256]{0,2,1:T(8,128)S(1)} fusion(bf16[2,256,5376]{2,1,0:T(8,128)(2,1)} %bitcast.137, bf16[1,512,5376]{2,1,0:T(8,128)(2,1)} %param.8, f32[5376]{0:T(1024)S(1)} %copy-done.7, f32[512]{0:T(512)S(1)} %add_rsqrt_fusion.1), kind=kOutput, calls=%fused_computation.37 | convolution fusion | flops 2829582336 | bytes 12082176 | tf_op jit(solution)/shard_map/dot_general | solution.py:94
  184.8 2.3 fusion.47
  187.1 41.6 %all-gather.8.cloned.1.call-done = bf16[5376,512]{1,0:T(8,128)(2,1)} async-done(((bf16[168,512]{1,0:T(8,128)(2,1)}), bf16[5376,512]{1,0:T(8,128)(2,1)}) %all-gather.8.cloned.1.call-update) | async-done | bytes 5505040 | tf_op jit(solution)/shard_map/all_gather | solution.py:79
  228.7 7.4 %convolution_convert_fusion.2 = bf16[512,5376]{1,0:T(8,128)(2,1)} fusion(bf16[512,512]{0,1:T(8,128)(2,1)S(1)} %bitcast.142, bf16[5376,512]{1,0:T(8,128)(2,1)} %all-gather.8.cloned.1.call-done), kind=kOutput, calls=%fused_computation.26 | convolution fusion | flops 2821324800 | bytes 11534336 | tf_op jit(solution)/shard_map/te,de->td/dot_general | solution.py:134
  237.7 111.0 %all-reduce.2.cloned.1.call-done = bf16[512,5376]{1,0:T(8,128)(2,1)} async-done(((bf16[512,5376]{1,0:T(8,128)(2,1)}), bf16[512,5376]{1,0:T(8,128)(2,1)}) %all-reduce.2.cloned.1.call-update) | async-done | bytes 5505040 | tf_op jit(solution)/shard_map/psum | solution.py:137
  348.6 3.9 fusion.15
  352.5 4.9 collective-permute-done.4
  357.4 7.1 %fusion.16 = (f32[512]{0:T(512)S(1)}, bf16[512,5376]{1,0:T(8,128)(2,1)S(1)}) fusion(bf16[512,5376]{1,0:T(8,128)(2,1)S(1)} %copy-done, bf16[512,5376]{1,0:T(8,128)(2,1)} %collective-permute-done.4, f32[5376]{0:T(1024)S(1)} %broadcast_multiply_fusion.1, f32[5376]{0:T(1024)S(1)} %copy-done.6, f32[512]{0:T(512)S(1)} %add_rsqrt_fusion, bf16[1,512,5376]{2,1,0:T(8,128)(2,1)} %param.8), kind=kLoop, calls=%fused_computation.21 | loop fusion | flops 33029632 | bytes 22067200 | tf_op jit(solution)/shard_map/reduce_sum | solution.py:142
  364.5 7.8 %fusion.8 = bf16[512,5376]{1,0:T(8,128)(2,1)S(1)} fusion(bf16[512,5376]{1,0:T(8,128)(2,1)S(1)} %copy-done, bf16[512,5376]{1,0:T(8,128)(2,1)} %collective-permute-done.4, bf16[512,5376]{1,0:T(8,128)(2,1)S(1)} %get-tuple-element.13, f32[512]{0:T(512)S(1)} %broadcast_multiply_fusion.2, f32[5376]{0:T(1024)S(1)} %broadcast_multiply_fusion.1, f32[512]{0:T(512)S(1)} %add_rsqrt_fusion), kind=kLoop, calls=%fused_computation.13 | loop fusion | flops 33030144 | bytes 22045696 | tf_op jit(solution)/shard_map/convert_element_type | solution.py:145
  372.4 3.5 convolution_convert_fusion
  375.8 5.8 convolution_convert_fusion.3
  381.6 2.3 fusion.17
  384.0 2.7 fusion.44
  387.0 3.6 convolution_convert_fusion.1
  390.6 5.1 pad_maximum_fusion
  395.7 14.7 %copy.48 = bf16[5376,1024]{1,0:T(8,128)(2,1)} copy(bf16[5376,1024]{0,1:T(8,128)(2,1)} %pad_maximum_fusion) | data formatting | bytes 22020096
  410.4 2.3 constant_dynamic-slice_fusion
  412.7 1.5 copy.35
  414.2 164.7 %reduce-scatter.4.cloned.1.call-done = bf16[168,1024]{1,0:T(8,128)(2,1)} async-done(((bf16[5376,1024]{1,0:T(8,128)(2,1)}), bf16[168,1024]{1,0:T(8,128)(2,1)}) %reduce-scatter.4.cloned.1.call-update) | async-done | bytes 344080
  (63 shorter events, 15.1 us)
Async XLA Ops:
  7.2 89.9 %all-gather.4.cloned.1.call-start = ((), (), s32[]{:S(2)}) async-start(), calls=%async_computation.2 | async-start | bytes 2838528 | tf_op jit(solution)/shard_map/all_gather | solution.py:78
  7.9 157.2 %all-gather.6.cloned.1.call-start = ((), (), s32[]{:S(2)}) async-start(), calls=%async_computation.3 | async-start | bytes 5677056 | tf_op jit(solution)/shard_map/all_gather | solution.py:71
  8.6 220.1 %all-gather.8.cloned.1.call-start = ((), (), s32[]{:S(2)}) async-start(), calls=%async_computation.4 | async-start | bytes 5677056 | tf_op jit(solution)/shard_map/all_gather | solution.py:79
  12.0 47.1 %all-to-all-start = ((bf16[32,168,256]{2,1,0:T(8,128)(2,1)}), bf16[32,168,256]{2,1,0:T(8,128)(2,1)S(1)}, u32[]{:S(2)}, u32[]{:S(2)}) async-start(bf16[32,168,256]{2,1,0:T(8,128)(2,1)} %stack.2), calls=%async_computation | async-start | bytes 5505024 | tf_op jit(solution)/shard_map/all_to_all | solution.py:73
  20.3 328.3 %all-reduce.2.cloned.1.call-start = ((), (), s32[]{:S(2)}) async-start(), calls=%async_computation.5 | async-start | bytes 11010048 | tf_op jit(solution)/shard_map/psum | solution.py:137
  64.8 115.9 %collective-permute-start.3 = (bf16[512,256]{0,1:T(8,128)(2,1)S(1)}, bf16[512,256]{0,1:T(8,128)(2,1)S(1)}, u32[]{:S(2)}, u32[]{:S(2)}) collective-permute-start(bf16[512,256]{0,1:T(8,128)(2,1)S(1)} %maximum_bitcast_fusion.6), channel_id=1, source_target_pairs={{0,4},{4,8},{8,12},{12,16},{16,20},{20,24},{24,28},{28,32},{32,36}... | collective-permute-start | bytes 786440 | tf_op jit(solution)/shard_map/ppermute | solution.py:29
  66.1 114.6 %collective-permute-start.2 = (bf16[512,256]{0,1:T(8,128)(2,1)S(1)}, bf16[512,256]{0,1:T(8,128)(2,1)S(1)}, u32[]{:S(2)}, u32[]{:S(2)}) collective-permute-start(bf16[512,256]{0,1:T(8,128)(2,1)S(1)} %maximum_bitcast_fusion.6), channel_id=1, source_target_pairs={{0,8},{4,12},{8,16},{12,20},{16,24},{20,28},{24,32},{28,36},{32,40... | collective-permute-start | bytes 786440 | tf_op jit(solution)/shard_map/ppermute | solution.py:29
  102.2 71.3 %copy-start.7 = (f32[5376]{0:T(1024)S(1)}, f32[5376]{0:T(1024)}, u32[]{:S(2)}) copy-start(f32[5376]{0:T(1024)} %param.10) | copy-start | bytes 64516
  102.2 81.5 %collective-permute-start.1 = (bf16[512,256]{1,0:T(8,128)(2,1)S(1)}, bf16[512,256]{1,0:T(8,128)(2,1)S(1)}, u32[]{:S(2)}, u32[]{:S(2)}) collective-permute-start(bf16[512,256]{1,0:T(8,128)(2,1)S(1)} %fusion.53), channel_id=1, source_target_pairs={{0,4},{4,8},{8,12},{12,16},{16,20},{20,24},{24,28},{28,32},{32,36}... | collective-permute-start | bytes 786440 | tf_op jit(solution)/shard_map/ppermute | solution.py:29
  104.3 79.3 %collective-permute-start = (bf16[512,256]{1,0:T(8,128)(2,1)S(1)}, bf16[512,256]{1,0:T(8,128)(2,1)S(1)}, u32[]{:S(2)}, u32[]{:S(2)}) collective-permute-start(bf16[512,256]{1,0:T(8,128)(2,1)S(1)} %fusion.53), channel_id=1, source_target_pairs={{0,8},{4,12},{8,16},{12,20},{16,24},{20,28},{24,32},{28,36},{32,40... | collective-permute-start | bytes 786440 | tf_op jit(solution)/shard_map/ppermute | solution.py:29
  173.5 7.0 %copy-start.3 = (f32[512,128]{0,1:T(8,128)S(1)}, f32[512,128]{0,1:T(8,128)}, u32[]{:S(2)}) copy-start(f32[512,128]{0,1:T(8,128)} %get-tuple-element.24) | copy-start | bytes 786436
  173.5 7.0 %copy-start.5 = (f32[512,128]{0,1:T(8,128)S(1)}, f32[512,128]{0,1:T(8,128)}, u32[]{:S(2)}) copy-start(f32[512,128]{0,1:T(8,128)} %get-tuple-element.23) | copy-start | bytes 786436
  182.1 2.7 copy-start.2
  228.7 9.0 %copy-start.6 = (f32[5376]{0:T(1024)S(1)}, f32[5376]{0:T(1024)}, u32[]{:S(2)}) copy-start(f32[5376]{0:T(1024)} %param.11) | copy-start | bytes 64516
  236.2 342.7 %reduce-scatter.4.cloned.1.call-start = ((), (), s32[]{:S(2)}) async-start(), calls=%async_computation.6 | async-start | bytes 11354112
  236.2 121.2 %collective-permute-start.4 = (bf16[512,5376]{1,0:T(8,128)(2,1)}, bf16[512,5376]{1,0:T(8,128)(2,1)}, u32[]{:S(2)}, u32[]{:S(2)}) collective-permute-start(bf16[512,5376]{1,0:T(8,128)(2,1)} %bitcast.141), channel_id=1, source_target_pairs={{0,64},{64,0},{1,65},{65,1},{2,66},{66,2},{3,67},{67,3},{4,68},{68... | collective-permute-start | bytes 16515080 | tf_op jit(solution)/shard_map/ppermute | solution.py:23
  348.6 8.8 %copy-start = (bf16[512,5376]{1,0:T(8,128)(2,1)S(1)}, bf16[512,5376]{1,0:T(8,128)(2,1)}, u32[]{:S(2)}) copy-start(bf16[512,5376]{1,0:T(8,128)(2,1)} %all-reduce.2.cloned.1.call-done) | copy-start | bytes 16515076
  364.5 7.9 %copy-start.1 = (bf16[512,5376]{1,0:T(8,128)(2,1)}, bf16[512,5376]{1,0:T(8,128)(2,1)S(1)}, u32[]{:S(2)}) copy-start(bf16[512,5376]{1,0:T(8,128)(2,1)S(1)} %get-tuple-element.13) | copy-start | bytes 16515076
  372.4 9.2 %slice-start.2 = ((s8[6291456]{0:T(1024)(128)(4,1)}), s8[4194304]{0:T(1024)(128)(4,1)S(1)}, s32[]{:S(2)}) async-start(s8[6291456]{0:T(1024)(128)(4,1)} %bitcast.134), calls=%async_computation.9 | async-start | bytes 8388608
  375.8 5.8 slice-start.3
  381.6 5.3 slice-start
  384.0 2.7 copy-start.4
  384.0 3.0 slice-start.1
Sparse Core Ops, SparseCore 0:
  9.7 87.3 all-gather.3
  98.8 66.2 all-gather.5
  166.8 61.8 all-gather.7
  236.3 112.3 all-reduce.1
  410.5 168.3 reduce-scatter.3
